TPU v7x, 32 devices: a whole 2x2x4 slice. The times are simulated.
32 devices in a mesh: gx: 8 (over z, y), gy: 4 (over x, core).
Axes of the slice: x: 2, y: 2, z: 4, core: 2. Of those that a mesh axis runs over, the one named last changes fastest.
Arguments:
- scalars: float32 [20, 64, 64, 128], P(None, 'gx', 'gy'), may hold values from -6 to 6
- velocity: float32 [3, 64, 64, 128], P(None, 'gx', 'gy'), may hold values from -4 to 4
- diffusivity: float32 [64, 64, 128], P('gx', 'gy'), may hold values from 0.05 to 0.6
- burn_list: int32 [8, 4, 64], P('gx', 'gy'), may hold values from 0 to 128, as said below
- w_in: bfloat16 [800, 20], replicated, may hold values from -1.25 to 1.25
- w_mid: bfloat16 [400, 800], replicated, may hold values from -0.21875 to 0.21875
- w_out: bfloat16 [20, 400], replicated, may hold values from -0.3125 to 0.3125
Outputs:
- scalars_out: float32 [20, 64, 64, 128], P(None, 'gx', 'gy')
- velocity_out: float32 [3, 64, 64, 128], P(None, 'gx', 'gy')
Inputs may be any that keep to these rules, and one draw needn't show every extreme that they name: `burn_list`: in each device's list the burning columns come first, distinct, and the remaining slots hold 128. A device lists 0 to 64 burning columns; in every group of devices with one gx index one device lists 64 and one lists none, and the group lists exactly 128 together.
All inputs are finite; a program needn't handle non-finite values.
Results may differ from a plain program's by a relative error of at most 0.0023.
Values may be sent and summed in bfloat16 or wider, within the bound.
A program may use at most 64 MiB of HBM per device.

v0:
```python
import functools
import math

import jax
import jax.numpy as jnp
import numpy as np
from jax import lax
from jax.experimental import pallas as pl
from jax.experimental.pallas import tpu as pltpu
from jax.sharding import PartitionSpec as P

time_step = 0.25


def with_halo(block, sides, width):
    for axis, dim in sides:
        count = lax.axis_size(axis)
        forward = [(i, i + 1) for i in range(count - 1)]
        forward.append((count - 1, 0))
        backward = [(target, source) for source, target in forward]
        low = lax.ppermute(
            lax.slice_in_dim(block, block.shape[dim] - width, None, axis=dim), axis, forward
        )
        high = lax.ppermute(lax.slice_in_dim(block, 0, width, axis=dim), axis, backward)
        block = jnp.concatenate([low, block, high], axis=dim)
    return block


def hartley_table(length):
    position = jnp.arange(length, dtype=jnp.int32)
    product = position[:, None] * position[None, :] % length
    phase_angle = 2.0 * math.pi / length * product.astype(jnp.float32)
    return (jnp.cos(phase_angle) + jnp.sin(phase_angle)) / math.sqrt(length)


def cosine_table(length):
    position = jnp.arange(length, dtype=jnp.int32)
    product = position[:, None] * (2 * position[None, :] + 1) % (4 * length)
    phase_angle = math.pi / (2 * length) * product.astype(jnp.float32)
    weight = jnp.where(position == 0, math.sqrt(1.0 / length), math.sqrt(2.0 / length)).astype(
        jnp.float32
    )
    return weight[:, None] * jnp.cos(phase_angle)


def depth_next(values):
    return jnp.concatenate([values[..., 1:], values[..., -1:]], -1)


def depth_prev(values):
    return jnp.concatenate([values[..., :1], values[..., :-1]], -1)


def transport_rate(field_pad, flow_pad):
    center = field_pad[:, 1:-1, 1:-1]
    x_next = field_pad[:, 2:, 1:-1]
    x_prev = field_pad[:, :-2, 1:-1]
    y_next = field_pad[:, 1:-1, 2:]
    y_prev = field_pad[:, 1:-1, :-2]
    z_next = depth_next(center)
    z_prev = depth_prev(center)
    coefficient = flow_pad[3, 1:-1, 1:-1]
    advection = (
        flow_pad[0, 1:-1, 1:-1] * (x_next - x_prev) * 0.5
        + flow_pad[1, 1:-1, 1:-1] * (y_next - y_prev) * 0.5
        + flow_pad[2, 1:-1, 1:-1] * (z_next - z_prev) * 0.5
    )
    diffusion = 0.5 * (coefficient + flow_pad[3, 2:, 1:-1]) * (x_next - center) - 0.5 * (
        coefficient + flow_pad[3, :-2, 1:-1]
    ) * (center - x_prev)
    diffusion = (
        diffusion
        + 0.5 * (coefficient + flow_pad[3, 1:-1, 2:]) * (y_next - center)
        - 0.5 * (coefficient + flow_pad[3, 1:-1, :-2]) * (center - y_prev)
    )
    diffusion = (
        diffusion
        + 0.5 * (coefficient + depth_next(coefficient)) * (z_next - center)
        - 0.5 * (coefficient + depth_prev(coefficient)) * (center - z_prev)
    )
    return diffusion - advection


def network(blocks, w_in, w_mid, w_out):
    block_count = blocks.shape[0]
    bundle_size = 8
    padded_count = -(-block_count // bundle_size) * bundle_size

    def evaluate(bundle):
        hidden_one = jnp.einsum("hn,bnz->bhz", w_in, bundle, preferred_element_type=jnp.float32)
        hidden_one = jax.nn.gelu(hidden_one).astype(jnp.bfloat16)
        hidden_two = jnp.einsum(
            "kh,bhz->bkz", w_mid, hidden_one, preferred_element_type=jnp.float32
        )
        hidden_two = jax.nn.gelu(hidden_two).astype(jnp.bfloat16)
        return jnp.einsum("nk,bkz->bnz", w_out, hidden_two, preferred_element_type=jnp.float32)

    reaction = lax.map(
        evaluate, blocks.reshape((padded_count // bundle_size, bundle_size) + blocks.shape[1:])
    )
    return reaction.reshape((padded_count,) + reaction.shape[2:])


def solve_modes(spectrum, start_y, start_z, total_x, total_y, total_z):
    mode_x = jnp.arange(spectrum.shape[0], dtype=jnp.int32)
    mode_y = start_y + jnp.arange(spectrum.shape[1], dtype=jnp.int32)
    mode_z = start_z + jnp.arange(spectrum.shape[2], dtype=jnp.int32)
    eigen_x = 2.0 - 2.0 * jnp.cos(2.0 * math.pi / total_x * mode_x.astype(jnp.float32))
    eigen_y = 2.0 - 2.0 * jnp.cos(2.0 * math.pi / total_y * mode_y.astype(jnp.float32))
    eigen_z = 2.0 - 2.0 * jnp.cos(math.pi / total_z * mode_z.astype(jnp.float32))
    eigen = eigen_x[:, None, None] + eigen_y[None, :, None] + eigen_z[None, None, :]
    anchor = (
        (mode_x[:, None, None] == 0) & (mode_y[None, :, None] == 0) & (mode_z[None, None, :] == 0)
    ).astype(jnp.float32)
    return -spectrum * (1.0 - anchor) / (eigen + anchor)


def shards(scalars, velocity, diffusivity, burn_list, w_in, w_mid, w_out):
    channels = scalars.shape[0]
    joined = jnp.concatenate([scalars, velocity, diffusivity[None]], 0)
    padded = with_halo(joined, (("gx", 1), ("gy", 2)), 1)
    field_pad = padded[:channels]
    inner_flow = padded[channels:]
    section_one = scalars + time_step * transport_rate(field_pad, inner_flow)
    section_pad = with_halo(section_one, (("gx", 1), ("gy", 2)), 1)
    transported = 0.5 * scalars + 0.5 * (
        section_one + time_step * transport_rate(section_pad, inner_flow)
    )
    divergence = 0.5 * (inner_flow[0, 2:, 1:-1] - inner_flow[0, :-2, 1:-1])
    divergence = divergence + 0.5 * (inner_flow[1, 1:-1, 2:] - inner_flow[1, 1:-1, :-2])
    vertical = inner_flow[2, 1:-1, 1:-1]
    divergence = divergence + 0.5 * (depth_next(vertical) - depth_prev(vertical))
    highest = lax.Precision.HIGHEST
    cells_x, cells_y, depth = divergence.shape
    total_x = cells_x * lax.axis_size("gx")
    total_y = cells_y * lax.axis_size("gy")
    table_x = hartley_table(total_x)
    table_y = hartley_table(total_y)
    table_z = cosine_table(depth)
    spectrum = jnp.einsum("az,xyz->xya", table_z, divergence, precision=highest)
    along_y = lax.all_to_all(spectrum, "gy", split_axis=2, concat_axis=1, tiled=True)
    along_y = jnp.einsum("by,xyz->xbz", table_y, along_y, precision=highest)
    along_x = lax.all_to_all(
        along_y.astype(jnp.bfloat16), "gx", split_axis=1, concat_axis=0, tiled=True
    ).astype(along_y.dtype)
    along_x = jnp.einsum("cx,xyz->cyz", table_x, along_x, precision=highest)
    solved = solve_modes(
        along_x,
        lax.axis_index("gx") * along_x.shape[1],
        lax.axis_index("gy") * along_x.shape[2],
        total_x,
        total_y,
        depth,
    )
    solved = jnp.einsum("cx,xyz->cyz", table_x, solved, precision=highest)
    solved = lax.all_to_all(solved, "gx", split_axis=0, concat_axis=1, tiled=True)
    solved = jnp.einsum("by,xyz->xbz", table_y, solved, precision=highest)
    solved = lax.all_to_all(solved, "gy", split_axis=1, concat_axis=2, tiled=True)
    pressure = jnp.einsum("az,xya->xyz", table_z, solved, precision=highest)
    pressure_pad = with_halo(pressure, (("gx", 0), ("gy", 1)), 1)
    grad_x = 0.5 * (pressure_pad[2:, 1:-1] - pressure_pad[:-2, 1:-1])
    grad_y = 0.5 * (pressure_pad[1:-1, 2:] - pressure_pad[1:-1, :-2])
    grad_z = 0.5 * (depth_next(pressure) - depth_prev(pressure))
    velocity_out = velocity - jnp.stack([grad_x, grad_y, grad_z])
    block_total = cells_x * cells_y
    flat_blocks = transported.reshape(channels, block_total, depth)
    listed = burn_list.reshape(-1)
    picked = jnp.take(flat_blocks, jnp.minimum(listed, block_total - 1), axis=1)
    chosen = jnp.transpose(picked, (1, 0, 2)).astype(jnp.bfloat16)
    own_rates = network(chosen, w_in, w_mid, w_out)
    updated = flat_blocks.at[:, listed].add(jnp.transpose(own_rates, (1, 0, 2)), mode="drop")
    scalars_out = updated.reshape(transported.shape)
    return (scalars_out, velocity_out)


MESH = pl.DeviceIdType.MESH
BUNDLE = 8


def hartley_np(length):
    product = np.outer(np.arange(length), np.arange(length)) % length
    angle = 2.0 * np.pi / length * product
    return (np.cos(angle) + np.sin(angle)) / np.sqrt(length)


def cosine_np(length):
    k = np.arange(length)
    angle = np.pi / (2 * length) * (np.outer(k, 2 * k + 1) % (4 * length))
    weight = np.where(k == 0, np.sqrt(1.0 / length), np.sqrt(2.0 / length))
    return weight[:, None] * np.cos(angle)


def split_np(table):
    high = table.astype(jnp.bfloat16)
    low = (table - high.astype(np.float64)).astype(jnp.bfloat16)
    return high, low


def split(value):
    high = value.astype(jnp.bfloat16)
    return high, (value - high.astype(jnp.float32)).astype(jnp.bfloat16)


def dot3(a, b, dims=((1,), (0,))):
    run = lambda p, q: lax.dot_general(p, q, (dims, ((), ())), preferred_element_type=jnp.float32)
    return run(a[0], b[0]) + (run(a[1], b[0]) + run(a[0], b[1]))


def z_neighbours(f):
    axis = f.ndim - 1
    depth = f.shape[axis]
    z = lax.broadcasted_iota(jnp.int32, f.shape, axis)
    after = jnp.where(z == depth - 1, f, pltpu.roll(f, depth - 1, axis))
    before = jnp.where(z == 0, f, pltpu.roll(f, 1, axis))
    return after, before


def y_neighbours(f, low, high):
    count = f.shape[1]
    y = lax.broadcasted_iota(jnp.int32, f.shape, 1)
    after = jnp.where(y == count - 1, high[:, None, :], pltpu.roll(f, count - 1, 1))
    before = jnp.where(y == 0, low[:, None, :], pltpu.roll(f, 1, 1))
    return after, before


def x_neighbours(f, low, high):
    after = jnp.concatenate([f[1:], high[None]], 0)
    before = jnp.concatenate([low[None], f[:-1]], 0)
    return after, before


def gelu(x):
    c = math.sqrt(2.0 / math.pi)
    inner = x * (c + (c * 0.044715) * (x * x))
    h = 0.5 * x
    return h + h * jnp.tanh(inner)


def grouped(count, size, body):
    size = size if count % size == 0 else 1

    def go(g, carry):
        for s in range(size):
            body(g * size + s)
        return carry

    lax.fori_loop(0, count // size, go, 0)


def step_kernel(
    ngx, ngy,
    scal_hbm, vel_hbm, dif_hbm, list_hbm, win_hbm, wmid_hbm, wout_hbm,
    exy_hbm, ez_hbm, czh_hbm, czl_hbm, tyh_hbm, tyl_hbm, txh_hbm, txl_hbm,
    out, vout,
    scal, vel, dif, listed, w_in, w_mid, w_out, exy, ez, cz_h, cz_l, ty_h, ty_l, tx_h, tx_l,
    xsend, ysend, xrecv, yrecv,
    x2send, y2send, x2recv, y2recv,
    psx, psy, prx, pry,
    coef, section, asend, arecv, bsend, brecv, plane, modes, feeds, rates,
    in_sem, h_sem, h2_sem, p_sem, a_sem, b_sem,
):
    channels, cx, cy, nz = scal.shape
    n = ngx * ngy
    kc = nz // n
    cells = cx * cy
    slots = listed.shape[1]
    f32, bf16 = jnp.float32, jnp.bfloat16
    i = lax.axis_index("gx")
    j = lax.axis_index("gy")
    me = i * ngy + j
    up_x = (lax.rem(i + 1, ngx), j)
    down_x = (lax.rem(i + ngx - 1, ngx), j)
    up_y = (i, lax.rem(j + 1, ngy))
    down_y = (i, lax.rem(j + ngy - 1, ngy))

    sources = (vel_hbm, dif_hbm, scal_hbm, list_hbm, czh_hbm, czl_hbm, ez_hbm.at[me], exy_hbm,
               tyh_hbm, tyl_hbm, txh_hbm, txl_hbm, win_hbm, wmid_hbm, wout_hbm)
    targets = (vel, dif, scal, listed, cz_h, cz_l, ez, exy,
               ty_h, ty_l, tx_h, tx_l, w_in, w_mid, w_out)
    fetches = [
        pltpu.make_async_copy(a, b, in_sem.at[at]) for at, (a, b) in enumerate(zip(sources, targets))
    ]
    for fetch in fetches:
        fetch.start()

    columns = [lax.rem(j + dj, ngy) for dj in range(ngy)]

    def others(fn):
        for dj in range(1, ngy):
            fn(i, columns[dj])

        def row(di, carry):
            i2 = lax.rem(i + di, ngx)
            for dj in range(ngy):
                fn(i2, columns[dj])
            return carry

        lax.fori_loop(1, ngx, row, 0)

    barrier = pltpu.get_barrier_semaphore()
    others(lambda i2, j2: pl.semaphore_signal(barrier, inc=1, device_id=(i2, j2), device_id_type=MESH))

    for fetch in fetches[:3]:
        fetch.wait()
    xsend[0, :channels] = scal[:, cx - 1]
    xsend[1, :channels] = scal[:, 0]
    ysend[0, :channels] = scal[:, :, cy - 1, :]
    ysend[1, :channels] = scal[:, :, 0, :]
    xsend[0, channels:channels + 3] = vel[:, cx - 1]
    xsend[1, channels:channels + 3] = vel[:, 0]
    ysend[0, channels:channels + 3] = vel[:, :, cy - 1, :]
    ysend[1, channels:channels + 3] = vel[:, :, 0, :]
    xsend[0, channels + 3] = dif[cx - 1]
    xsend[1, channels + 3] = dif[0]
    ysend[0, channels + 3] = dif[:, cy - 1, :]
    ysend[1, channels + 3] = dif[:, 0, :]
    pl.semaphore_wait(barrier, n - 1)

    def halo(xs, ys, xr, yr, sems):
        copies = []
        plan = ((xs, xr, 0, up_x), (xs, xr, 1, down_x), (ys, yr, 0, up_y), (ys, yr, 1, down_y))
        for at, (s, r, side, target) in enumerate(plan):
            copy = pltpu.make_async_remote_copy(
                src_ref=s.at[side], dst_ref=r.at[side], send_sem=sems.at[0, at],
                recv_sem=sems.at[1, at], device_id=target, device_id_type=MESH,
            )
            copy.start()
            copies.append(copy)
        return copies

    def everyone(send, recv, sems):
        def go(i2, j2):
            pltpu.make_async_remote_copy(
                src_ref=send.at[i2 * ngy + j2], dst_ref=recv.at[me], send_sem=sems.at[0],
                recv_sem=sems.at[1], device_id=(i2, j2), device_id_type=MESH,
            ).start()

        others(go)
        recv[me] = send[me]

    def everyone_wait(recv, sems, side):
        part = recv.at[pl.ds(0, n - 1)]
        pltpu.make_async_copy(part, part, sems.at[side]).wait()

    first_halo = halo(xsend, ysend, xrecv, yrecv, h_sem)
    for fetch in fetches[3:6]:
        fetch.wait()
    cell = lax.broadcasted_iota(jnp.int32, (cells, slots), 0)
    put = (cell == listed[...]).astype(f32)
    take = put.T.astype(bf16)
    put = jnp.concatenate([put, put], 1).astype(bf16)
    for copy in first_halo:
        copy.wait()

    u, v, w = vel[0], vel[1], vel[2]
    un, up = x_neighbours(u, xrecv[0, channels], xrecv[1, channels])
    vn, vp = y_neighbours(v, yrecv[0, channels + 1], yrecv[1, channels + 1])
    wn, wp = z_neighbours(w)
    div = 0.5 * (un - up) + 0.5 * (vn - vp) + 0.5 * (wn - wp)
    div = div.reshape(cells, nz)
    spec = dot3((cz_h[...], cz_l[...]), split(div), ((1,), (1,)))
    for d in range(n):
        asend[d] = spec[d * kc:(d + 1) * kc]
    everyone(asend, arecv, a_sem)

    k = dif[...]
    kxn, kxp = x_neighbours(k, xrecv[0, channels + 3], xrecv[1, channels + 3])
    kyn, kyp = y_neighbours(k, yrecv[0, channels + 3], yrecv[1, channels + 3])
    kzn, kzp = z_neighbours(k)
    half = 0.5 * time_step
    total = None
    for at, (nb, flow) in enumerate(((kxn, -u), (kxp, u), (kyn, -v), (kyp, v), (kzn, -w), (kzp, w))):
        face = k + nb
        coef[at] = half * (face + flow)
        total = face if total is None else total + face
    coef[6] = half * total

    def advance(f, xl, xh, yl, yh):
        xn, xp = x_neighbours(f, xl, xh)
        rate = coef[0] * xn + coef[1] * xp - coef[6] * f
        yn, yp = y_neighbours(f, yl, yh)
        rate = rate + (coef[2] * yn + coef[3] * yp)
        zn, zp = z_neighbours(f)
        return f + (rate + (coef[4] * zn + coef[5] * zp))

    def first(c):
        s = advance(scal[c], xrecv[0, c], xrecv[1, c], yrecv[0, c], yrecv[1, c])
        section[c] = s
        x2send[0, c] = s[cx - 1]
        x2send[1, c] = s[0]
        y2send[0, c] = s[:, cy - 1, :]
        y2send[1, c] = s[:, 0, :]

    grouped(channels, 2, first)
    second_halo = halo(x2send, y2send, x2recv, y2recv, h2_sem)

    for fetch in fetches[6:]:
        fetch.wait()
    rows = ngx * kc
    ny = cy * ngy
    eigen = exy[...] + jnp.concatenate([ez[...]] * (cx * rows // ez.shape[0]), 0)
    minv = jnp.where(eigen == 0.0, 0.0, -1.0 / jnp.where(eigen == 0.0, 1.0, eigen))
    everyone_wait(arecv, a_sem, 1)
    for d in range(n):
        a, b = divmod(d, ngy)
        plane[a * kc:(a + 1) * kc, b * cells:(b + 1) * cells] = arecv[d]
    table_y = (ty_h[...], ty_l[...])
    table_x = (tx_h[...], tx_l[...])
    along = dot3(split(plane[...]), table_y)
    along = jnp.concatenate([along[:, a * ny:(a + 1) * ny] for a in range(cx)], 0)
    along = dot3(table_x, split(along)) * minv
    along = dot3(table_x, split(along))
    along = jnp.concatenate([along[a * rows:(a + 1) * rows] for a in range(cx)], 1)
    along = dot3(split(along), table_y, ((1,), (1,)))
    for d in range(n):
        a, b = divmod(d, ngy)
        bsend[d] = along[a * kc:(a + 1) * kc, b * cells:(b + 1) * cells]
    everyone(bsend, brecv, b_sem)

    for copy in second_halo:
        copy.wait()

    def second(c):
        s = advance(section[c], x2recv[0, c], x2recv[1, c], y2recv[0, c], y2recv[1, c])
        t = 0.5 * scal[c] + 0.5 * s
        out[c] = t
        feeds[pl.ds(c * slots, slots), :] = jnp.dot(
            take, t.reshape(cells, nz).astype(bf16), preferred_element_type=f32
        )

    grouped(channels, 2, second)

    def react(g, carry):
        base = g * BUNDLE
        feed = jnp.concatenate(
            [feeds[pl.ds(base + s, channels, stride=slots), :] for s in range(BUNDLE)], 1
        ).astype(bf16)
        one = lax.dot_general(w_in[...], feed, (((0,), (0,)), ((), ())), preferred_element_type=f32)
        one = gelu(one).astype(bf16)
        two = gelu(jnp.dot(w_mid[...], one, preferred_element_type=f32)).astype(bf16)
        rate = jnp.dot(w_out[...], two, preferred_element_type=f32)
        for s in range(BUNDLE):
            rates[pl.ds(base + s, channels, stride=slots), :] = rate[:, s * nz:(s + 1) * nz]
        return carry

    bundles = slots // BUNDLE
    cut_one, cut_two = bundles * 3 // 8, bundles * 6 // 8
    lax.fori_loop(0, cut_one, react, 0)

    everyone_wait(brecv, b_sem, 1)
    for d in range(n):
        modes[d * kc:(d + 1) * kc] = brecv[d]
    pressure = dot3(split(modes[...].T), (cz_h[...], cz_l[...])).reshape(cx, cy, nz)
    psx[0] = pressure[cx - 1]
    psx[1] = pressure[0]
    psy[0] = pressure[:, cy - 1, :]
    psy[1] = pressure[:, 0, :]
    last = halo(psx, psy, prx, pry, p_sem)
    zn, zp = z_neighbours(pressure)
    vout[2] = vel[2] - 0.5 * (zn - zp)
    section[0] = pressure

    lax.fori_loop(cut_one, cut_two, react, 0)

    for copy in last:
        copy.wait()
    pressure = section[0]
    xn, xp = x_neighbours(pressure, prx[0], prx[1])
    vout[0] = vel[0] - 0.5 * (xn - xp)
    yn, yp = y_neighbours(pressure, pry[0], pry[1])
    vout[1] = vel[1] - 0.5 * (yn - yp)

    lax.fori_loop(cut_two, bundles, react, 0)

    def scatter(c):
        parts = jnp.concatenate(split(rates[pl.ds(c * slots, slots), :]), 0)
        added = jnp.dot(put, parts, preferred_element_type=f32)
        out[c] = out[c] + added.reshape(cx, cy, nz)

    grouped(channels, 4, scatter)
    everyone_wait(arecv, a_sem, 0)
    everyone_wait(brecv, b_sem, 0)


def fast_shards(scalars, velocity, diffusivity, burn_list, w_in, w_mid, w_out):
    ngx, ngy = lax.axis_size("gx"), lax.axis_size("gy")
    channels, cx, cy, nz = scalars.shape
    n = ngx * ngy
    kc = nz // n
    nx, ny = cx * ngx, cy * ngy
    hx, hy = hartley_np(nx), hartley_np(ny)
    ty = np.einsum("ab,cjy->jaybc", np.eye(cx), hy.reshape(ny, ngy, cy)).reshape(ngy * cx * cy, cx * ny)
    order = (np.arange(ngx)[None, :] * cx + np.arange(cx)[:, None]).reshape(-1)
    tx = np.kron(hx[np.ix_(order, order)], np.eye(kc))
    ex = np.repeat(2.0 - 2.0 * np.cos(2.0 * np.pi / nx * order), kc)
    ey = 2.0 - 2.0 * np.cos(2.0 * np.pi / ny * np.arange(ny))
    exy = (ex[:, None] + ey[None, :]).astype(np.float32)
    ez = 2.0 - 2.0 * np.cos(np.pi / nz * np.arange(nz))
    ez = np.tile(ez.reshape(n, kc, 1), (1, max(1, 8 // kc), ny)).astype(np.float32)
    tables = [t for pair in (split_np(cosine_np(nz)), split_np(ty), split_np(tx)) for t in pair]
    operands = [
        scalars, velocity, diffusivity, burn_list.reshape(1, -1), w_in.T, w_mid, w_out,
        *(jnp.asarray(t) for t in (exy, ez, *tables)),
    ]
    f32 = jnp.float32
    slots = operands[3].shape[1]
    vm = pl.BlockSpec(memory_space=pltpu.VMEM)
    copies = [pltpu.VMEM(a.shape, a.dtype) for a in operands]
    copies[8] = pltpu.VMEM(ez.shape[1:], f32)
    halo_scratch = lambda c: [pltpu.VMEM((2, c, cy, nz), f32), pltpu.VMEM((2, c, cx, nz), f32)]
    face_scratch = [pltpu.VMEM((2, cy, nz), f32), pltpu.VMEM((2, cx, nz), f32)]
    chunk = pltpu.VMEM((n, kc, cx * cy), f32)
    dma = pltpu.SemaphoreType.DMA
    return pl.pallas_call(
        functools.partial(step_kernel, ngx, ngy),
        out_shape=(jax.ShapeDtypeStruct(scalars.shape, f32), jax.ShapeDtypeStruct(velocity.shape, f32)),
        in_specs=[pl.BlockSpec(memory_space=pl.ANY)] * len(operands),
        out_specs=(vm, vm),
        scratch_shapes=copies + halo_scratch(channels + 4) * 2 + halo_scratch(channels) * 2 + face_scratch * 2 + [
            pltpu.VMEM((7, cx, cy, nz), f32), pltpu.VMEM(scalars.shape, f32),
            chunk, chunk, chunk, chunk,
            pltpu.VMEM((ngx * kc, ngy * cx * cy), f32), pltpu.VMEM((nz, cx * cy), f32),
            pltpu.VMEM((channels * slots, nz), f32), pltpu.VMEM((channels * slots, nz), f32),
            dma((len(operands),)), dma((2, 4)), dma((2, 4)), dma((2, 4)), dma((2,)), dma((2,)),
        ],
        compiler_params=pltpu.CompilerParams(
            collective_id=0, has_side_effects=True, vmem_limit_bytes=60 * 1024 * 1024
        ),
    )(*operands)


def local_shards(scalars, velocity, diffusivity, *rest):
    depth = scalars.shape[-1]
    devices = lax.axis_size("gx") * lax.axis_size("gy")
    whole_chunks = depth % devices == 0 and 8 % (depth // devices) == 0
    plan = fast_shards if whole_chunks else shards
    return plan(scalars, velocity, diffusivity, *rest)


def solution(mesh):
    in_specs = (
        P(None, "gx", "gy", None),
        P(None, "gx", "gy", None),
        P("gx", "gy", None),
        P("gx", "gy", None),
        P(),
        P(),
        P(),
    )
    out_specs = (P(None, "gx", "gy", None), P(None, "gx", "gy", None))
    return jax.shard_map(local_shards, mesh=mesh, in_specs=in_specs, out_specs=out_specs, check_vma=False)
```

profile of v0, /device:TPU:0, one launch (start us, length us, event | category | flops | bytes accessed | tf_op | source)
XLA Modules:
  0.0 54.8 jit_solution(8322642306830109091)
XLA Ops:
  0.6 50.9 %shard_map.158 = (f32[20,8,16,128]{3,2,1,0:T(8,128)}, f32[3,8,16,128]{3,2,1,0:T(8,128)}) custom-call(f32[20,8,16,128]{3,2,1,0:T(8,128)} %scal_hbm.1, f32[3,8,16,128]{3,2,1,0:T(8,128)} %vel_hbm.1, f32[8,16,128]{2,1,0:T(8,128)} %dif_hbm.1, s32[1,64]{1,0:T(1,128)} %bitcast.3, bf16[20,800]{1,0:T(8,128)(2,1)} %bitcast.2, bf16[400,800]{1,0:T(8,128)(2,1)} %wmid_hbm.1, ...), custom_call_target="tpu_custom_call" | custom-call | tf_op jit(solution)/shard_map/pallas_call | solution.py:514
  51.5 0.0 copy-start
  51.6 2.5 %copy.19 = f32[20,8,16,128]{3,2,1,0:T(8,128)} copy(f32[20,8,16,128]{3,2,1,0:T(8,128)} %get-tuple-element.4) | data formatting | bytes 2621440
  54.1 0.0 copy-done
  54.1 0.7 %copy.20 = f32[3,8,16,128]{3,2,1,0:T(8,128)} copy(f32[3,8,16,128]{3,2,1,0:T(8,128)S(1)} %copy-done) | data formatting | bytes 393216
Async XLA Ops:
  51.5 2.5 %copy-start = (f32[3,8,16,128]{3,2,1,0:T(8,128)S(1)}, f32[3,8,16,128]{3,2,1,0:T(8,128)}, u32[]{:S(2)}) copy-start(f32[3,8,16,128]{3,2,1,0:T(8,128)} %get-tuple-element.5) | copy-start | bytes 589828
where the time goes:
time: 54.9 us; the launch traced here: 54.8 us
  Pallas kernels  50.9 us (93%)
  local copies, waits for them, and re-layouts  3.21 us (6%)
  between operations  0.65 us (1%)
    pallas_call x1, Pallas kernels, fast_shards(): pl.pallas_call(functools.partial(step_kernel, ngx, ngy), out_shape=(jax.S...  50.9 us
    unnamed x4, local copies, waits for them, and re-layouts  3.21 us

commit v1 on v0

--- a/solution.py
+++ b/solution.py
@@ -255,9 +255,9 @@
     scal, vel, dif, listed, w_in, w_mid, w_out, exy, ez, cz_h, cz_l, ty_h, ty_l, tx_h, tx_l,
     xsend, ysend, xrecv, yrecv,
     x2send, y2send, x2recv, y2recv,
-    psx, psy, prx, pry,
+    psx, psy, prx, pry, gsx, gsy, grx, gry,
     coef, section, asend, arecv, bsend, brecv, plane, modes, feeds, rates,
-    in_sem, h_sem, h2_sem, p_sem, a_sem, b_sem,
+    in_sem, g_sem, h_sem, h2_sem, p_sem, a_sem, b_sem,
 ):
     channels, cx, cy, nz = scal.shape
     n = ngx * ngy
@@ -280,7 +280,7 @@
     fetches = [
         pltpu.make_async_copy(a, b, in_sem.at[at]) for at, (a, b) in enumerate(zip(sources, targets))
     ]
-    for fetch in fetches:
+    for fetch in fetches[:3]:
         fetch.start()
 
     columns = [lax.rem(j + dj, ngy) for dj in range(ngy)]
@@ -300,20 +300,23 @@
     barrier = pltpu.get_barrier_semaphore()
     others(lambda i2, j2: pl.semaphore_signal(barrier, inc=1, device_id=(i2, j2), device_id_type=MESH))
 
-    for fetch in fetches[:3]:
+    for fetch in fetches[:2]:
         fetch.wait()
-    xsend[0, :channels] = scal[:, cx - 1]
-    xsend[1, :channels] = scal[:, 0]
-    ysend[0, :channels] = scal[:, :, cy - 1, :]
-    ysend[1, :channels] = scal[:, :, 0, :]
-    xsend[0, channels:channels + 3] = vel[:, cx - 1]
-    xsend[1, channels:channels + 3] = vel[:, 0]
-    ysend[0, channels:channels + 3] = vel[:, :, cy - 1, :]
-    ysend[1, channels:channels + 3] = vel[:, :, 0, :]
-    xsend[0, channels + 3] = dif[cx - 1]
-    xsend[1, channels + 3] = dif[0]
-    ysend[0, channels + 3] = dif[:, cy - 1, :]
-    ysend[1, channels + 3] = dif[:, 0, :]
+    for side, at in ((0, cx - 1), (1, 0)):
+        gsx[side, 0] = vel[0, at]
+        gsx[side, 1] = dif[at]
+    for side, at in ((0, cy - 1), (1, 0)):
+        gsy[side, 0] = vel[1, :, at, :]
+        gsy[side, 1] = dif[:, at, :]
+    fetches[2].wait()
+
+    def pack(c, f, xs, ys):
+        xs[0, c] = f[cx - 1].astype(bf16)
+        xs[1, c] = f[0].astype(bf16)
+        ys[0, c] = f[:, cy - 1, :].astype(bf16)
+        ys[1, c] = f[:, 0, :].astype(bf16)
+
+    grouped(channels, 4, lambda c: pack(c, scal[c], xsend, ysend))
     pl.semaphore_wait(barrier, n - 1)
 
     def halo(xs, ys, xr, yr, sems):
@@ -342,19 +345,22 @@
         part = recv.at[pl.ds(0, n - 1)]
         pltpu.make_async_copy(part, part, sems.at[side]).wait()
 
+    flow_halo = halo(gsx, gsy, grx, gry, g_sem)
     first_halo = halo(xsend, ysend, xrecv, yrecv, h_sem)
+    for fetch in fetches[3:]:
+        fetch.start()
     for fetch in fetches[3:6]:
         fetch.wait()
     cell = lax.broadcasted_iota(jnp.int32, (cells, slots), 0)
     put = (cell == listed[...]).astype(f32)
     take = put.T.astype(bf16)
     put = jnp.concatenate([put, put], 1).astype(bf16)
-    for copy in first_halo:
+    for copy in flow_halo:
         copy.wait()
 
     u, v, w = vel[0], vel[1], vel[2]
-    un, up = x_neighbours(u, xrecv[0, channels], xrecv[1, channels])
-    vn, vp = y_neighbours(v, yrecv[0, channels + 1], yrecv[1, channels + 1])
+    un, up = x_neighbours(u, grx[0, 0], grx[1, 0])
+    vn, vp = y_neighbours(v, gry[0, 0], gry[1, 0])
     wn, wp = z_neighbours(w)
     div = 0.5 * (un - up) + 0.5 * (vn - vp) + 0.5 * (wn - wp)
     div = div.reshape(cells, nz)
@@ -364,8 +370,8 @@
     everyone(asend, arecv, a_sem)
 
     k = dif[...]
-    kxn, kxp = x_neighbours(k, xrecv[0, channels + 3], xrecv[1, channels + 3])
-    kyn, kyp = y_neighbours(k, yrecv[0, channels + 3], yrecv[1, channels + 3])
+    kxn, kxp = x_neighbours(k, grx[0, 1], grx[1, 1])
+    kyn, kyp = y_neighbours(k, gry[0, 1], gry[1, 1])
     kzn, kzp = z_neighbours(k)
     half = 0.5 * time_step
     total = None
@@ -375,7 +381,8 @@
         total = face if total is None else total + face
     coef[6] = half * total
 
-    def advance(f, xl, xh, yl, yh):
+    def advance(f, c, xr, yr):
+        xl, xh, yl, yh = (r[side, c].astype(f32) for r in (xr, yr) for side in (0, 1))
         xn, xp = x_neighbours(f, xl, xh)
         rate = coef[0] * xn + coef[1] * xp - coef[6] * f
         yn, yp = y_neighbours(f, yl, yh)
@@ -383,13 +390,13 @@
         zn, zp = z_neighbours(f)
         return f + (rate + (coef[4] * zn + coef[5] * zp))
 
+    for copy in first_halo:
+        copy.wait()
+
     def first(c):
-        s = advance(scal[c], xrecv[0, c], xrecv[1, c], yrecv[0, c], yrecv[1, c])
+        s = advance(scal[c], c, xrecv, yrecv)
         section[c] = s
-        x2send[0, c] = s[cx - 1]
-        x2send[1, c] = s[0]
-        y2send[0, c] = s[:, cy - 1, :]
-        y2send[1, c] = s[:, 0, :]
+        pack(c, s, x2send, y2send)
 
     grouped(channels, 2, first)
     second_halo = halo(x2send, y2send, x2recv, y2recv, h2_sem)
@@ -421,7 +428,7 @@
         copy.wait()
 
     def second(c):
-        s = advance(section[c], x2recv[0, c], x2recv[1, c], y2recv[0, c], y2recv[1, c])
+        s = advance(section[c], c, x2recv, y2recv)
         t = 0.5 * scal[c] + 0.5 * s
         out[c] = t
         feeds[pl.ds(c * slots, slots), :] = jnp.dot(
@@ -507,7 +514,7 @@
     vm = pl.BlockSpec(memory_space=pltpu.VMEM)
     copies = [pltpu.VMEM(a.shape, a.dtype) for a in operands]
     copies[8] = pltpu.VMEM(ez.shape[1:], f32)
-    halo_scratch = lambda c: [pltpu.VMEM((2, c, cy, nz), f32), pltpu.VMEM((2, c, cx, nz), f32)]
+    halo_scratch = lambda c, t: [pltpu.VMEM((2, c, cy, nz), t), pltpu.VMEM((2, c, cx, nz), t)]
     face_scratch = [pltpu.VMEM((2, cy, nz), f32), pltpu.VMEM((2, cx, nz), f32)]
     chunk = pltpu.VMEM((n, kc, cx * cy), f32)
     dma = pltpu.SemaphoreType.DMA
@@ -516,12 +523,12 @@
         out_shape=(jax.ShapeDtypeStruct(scalars.shape, f32), jax.ShapeDtypeStruct(velocity.shape, f32)),
         in_specs=[pl.BlockSpec(memory_space=pl.ANY)] * len(operands),
         out_specs=(vm, vm),
-        scratch_shapes=copies + halo_scratch(channels + 4) * 2 + halo_scratch(channels) * 2 + face_scratch * 2 + [
+        scratch_shapes=copies + halo_scratch(channels, jnp.bfloat16) * 4 + face_scratch * 2 + halo_scratch(2, f32) * 2 + [
             pltpu.VMEM((7, cx, cy, nz), f32), pltpu.VMEM(scalars.shape, f32),
             chunk, chunk, chunk, chunk,
             pltpu.VMEM((ngx * kc, ngy * cx * cy), f32), pltpu.VMEM((nz, cx * cy), f32),
             pltpu.VMEM((channels * slots, nz), f32), pltpu.VMEM((channels * slots, nz), f32),
-            dma((len(operands),)), dma((2, 4)), dma((2, 4)), dma((2, 4)), dma((2,)), dma((2,)),
+            dma((len(operands),)), dma((2, 4)), dma((2, 4)), dma((2, 4)), dma((2, 4)), dma((2,)), dma((2,)),
         ],
         compiler_params=pltpu.CompilerParams(
             collective_id=0, has_side_effects=True, vmem_limit_bytes=60 * 1024 * 1024

time: 54.9 us -> 46.8 us (0.85)
  Pallas kernels: 50.9 us -> 42.7 us
    pallas_call x1, Pallas kernels: 50.9 us -> 42.7 us  [fast_shards(): pl.pallas_call(functools.partial(step_kernel, ngx, ngy), out_shape=(jax.S...]
where the time goes in v1:
time: 46.8 us; the launch traced here: 46.6 us
  Pallas kernels  42.7 us (91%)
  local copies, waits for them, and re-layouts  3.21 us (7%)
  between operations  0.65 us (1%)
    pallas_call x1, Pallas kernels, fast_shards(): pl.pallas_call(functools.partial(step_kernel, ngx, ngy), out_shape=(jax.S...  42.7 us
    unnamed x4, local copies, waits for them, and re-layouts  3.21 us

profile of v1, /device:TPU:0, one launch (start us, length us, event | category | flops | bytes accessed | tf_op | source)
XLA Modules:
  0.0 46.6 jit_solution(5412367835848371045)
XLA Ops:
  0.6 42.7 %shard_map.158 = (f32[20,8,16,128]{3,2,1,0:T(8,128)}, f32[3,8,16,128]{3,2,1,0:T(8,128)}) custom-call(f32[20,8,16,128]{3,2,1,0:T(8,128)} %scal_hbm.1, f32[3,8,16,128]{3,2,1,0:T(8,128)} %vel_hbm.1, f32[8,16,128]{2,1,0:T(8,128)} %dif_hbm.1, s32[1,64]{1,0:T(1,128)} %bitcast.3, bf16[20,800]{1,0:T(8,128)(2,1)} %bitcast.2, bf16[400,800]{1,0:T(8,128)(2,1)} %wmid_hbm.1, ...), custom_call_target="tpu_custom_call" | custom-call | tf_op jit(solution)/shard_map/pallas_call | solution.py:521
  43.4 0.0 copy-start
  43.4 2.5 %copy.19 = f32[20,8,16,128]{3,2,1,0:T(8,128)} copy(f32[20,8,16,128]{3,2,1,0:T(8,128)} %get-tuple-element.4) | data formatting | bytes 2621440
  45.9 0.0 copy-done
  45.9 0.7 %copy.20 = f32[3,8,16,128]{3,2,1,0:T(8,128)} copy(f32[3,8,16,128]{3,2,1,0:T(8,128)S(1)} %copy-done) | data formatting | bytes 393216
Async XLA Ops:
  43.4 2.5 %copy-start = (f32[3,8,16,128]{3,2,1,0:T(8,128)S(1)}, f32[3,8,16,128]{3,2,1,0:T(8,128)}, u32[]{:S(2)}) copy-start(f32[3,8,16,128]{3,2,1,0:T(8,128)} %get-tuple-element.5) | copy-start | bytes 589828

commit v2 on v1

--- a/solution.py
+++ b/solution.py
@@ -443,7 +443,7 @@
             [feeds[pl.ds(base + s, channels, stride=slots), :] for s in range(BUNDLE)], 1
         ).astype(bf16)
         one = lax.dot_general(w_in[...], feed, (((0,), (0,)), ((), ())), preferred_element_type=f32)
-        one = gelu(one).astype(bf16)
+        one = gelu(one.astype(bf16))
         two = gelu(jnp.dot(w_mid[...], one, preferred_element_type=f32)).astype(bf16)
         rate = jnp.dot(w_out[...], two, preferred_element_type=f32)
         for s in range(BUNDLE):

time: 46.8 us -> 44.8 us (0.957)
  Pallas kernels: 42.7 us -> 40.7 us
    pallas_call x1, Pallas kernels: 42.7 us -> 40.7 us  [fast_shards(): pl.pallas_call(functools.partial(step_kernel, ngx, ngy), out_shape=(jax.S...]
where the time goes in v2:
time: 44.8 us; the launch traced here: 44.6 us
  Pallas kernels  40.7 us (91%)
  local copies, waits for them, and re-layouts  3.21 us (7%)
  between operations  0.65 us (1%)
    pallas_call x1, Pallas kernels, fast_shards(): pl.pallas_call(functools.partial(step_kernel, ngx, ngy), out_shape=(jax.S...  40.7 us
    unnamed x4, local copies, waits for them, and re-layouts  3.21 us

profile of v2, /device:TPU:0, one launch (start us, length us, event | category | flops | bytes accessed | tf_op | source)
XLA Modules:
  0.0 44.6 jit_solution(2961515698425850342)
XLA Ops:
  0.6 40.7 %shard_map.158 = (f32[20,8,16,128]{3,2,1,0:T(8,128)}, f32[3,8,16,128]{3,2,1,0:T(8,128)}) custom-call(f32[20,8,16,128]{3,2,1,0:T(8,128)} %scal_hbm.1, f32[3,8,16,128]{3,2,1,0:T(8,128)} %vel_hbm.1, f32[8,16,128]{2,1,0:T(8,128)} %dif_hbm.1, s32[1,64]{1,0:T(1,128)} %bitcast.3, bf16[20,800]{1,0:T(8,128)(2,1)} %bitcast.2, bf16[400,800]{1,0:T(8,128)(2,1)} %wmid_hbm.1, ...), custom_call_target="tpu_custom_call" | custom-call | tf_op jit(solution)/shard_map/pallas_call | solution.py:521
  41.4 0.0 copy-start
  41.4 2.5 %copy.19 = f32[20,8,16,128]{3,2,1,0:T(8,128)} copy(f32[20,8,16,128]{3,2,1,0:T(8,128)} %get-tuple-element.4) | data formatting | bytes 2621440
  43.9 0.0 copy-done
  43.9 0.7 %copy.20 = f32[3,8,16,128]{3,2,1,0:T(8,128)} copy(f32[3,8,16,128]{3,2,1,0:T(8,128)S(1)} %copy-done) | data formatting | bytes 393216
Async XLA Ops:
  41.4 2.5 %copy-start = (f32[3,8,16,128]{3,2,1,0:T(8,128)S(1)}, f32[3,8,16,128]{3,2,1,0:T(8,128)}, u32[]{:S(2)}) copy-start(f32[3,8,16,128]{3,2,1,0:T(8,128)} %get-tuple-element.5) | copy-start | bytes 589828

commit v3 on v2

--- a/solution.py
+++ b/solution.py
@@ -444,7 +444,7 @@
         ).astype(bf16)
         one = lax.dot_general(w_in[...], feed, (((0,), (0,)), ((), ())), preferred_element_type=f32)
         one = gelu(one.astype(bf16))
-        two = gelu(jnp.dot(w_mid[...], one, preferred_element_type=f32)).astype(bf16)
+        two = gelu(jnp.dot(w_mid[...], one, preferred_element_type=f32).astype(bf16))
         rate = jnp.dot(w_out[...], two, preferred_element_type=f32)
         for s in range(BUNDLE):
             rates[pl.ds(base + s, channels, stride=slots), :] = rate[:, s * nz:(s + 1) * nz]

time: 44.8 us -> 43.4 us (0.969)
  Pallas kernels: 40.7 us -> 39.3 us
    pallas_call x1, Pallas kernels: 40.7 us -> 39.3 us  [fast_shards(): pl.pallas_call(functools.partial(step_kernel, ngx, ngy), out_shape=(jax.S...]
where the time goes in v3:
time: 43.4 us; the launch traced here: 43.2 us
  Pallas kernels  39.3 us (91%)
  local copies, waits for them, and re-layouts  3.21 us (7%)
  between operations  0.65 us (1%)
    pallas_call x1, Pallas kernels, fast_shards(): pl.pallas_call(functools.partial(step_kernel, ngx, ngy), out_shape=(jax.S...  39.3 us
    unnamed x4, local copies, waits for them, and re-layouts  3.21 us

profile of v3, /device:TPU:0, one launch (start us, length us, event | category | flops | bytes accessed | tf_op | source)
XLA Modules:
  0.0 43.2 jit_solution(17277620195438211338)
XLA Ops:
  0.6 39.3 %shard_map.158 = (f32[20,8,16,128]{3,2,1,0:T(8,128)}, f32[3,8,16,128]{3,2,1,0:T(8,128)}) custom-call(f32[20,8,16,128]{3,2,1,0:T(8,128)} %scal_hbm.1, f32[3,8,16,128]{3,2,1,0:T(8,128)} %vel_hbm.1, f32[8,16,128]{2,1,0:T(8,128)} %dif_hbm.1, s32[1,64]{1,0:T(1,128)} %bitcast.3, bf16[20,800]{1,0:T(8,128)(2,1)} %bitcast.2, bf16[400,800]{1,0:T(8,128)(2,1)} %wmid_hbm.1, ...), custom_call_target="tpu_custom_call" | custom-call | tf_op jit(solution)/shard_map/pallas_call | solution.py:521
  39.9 0.0 copy-start
  40.0 2.5 %copy.19 = f32[20,8,16,128]{3,2,1,0:T(8,128)} copy(f32[20,8,16,128]{3,2,1,0:T(8,128)} %get-tuple-element.4) | data formatting | bytes 2621440
  42.5 0.0 copy-done
  42.5 0.7 %copy.20 = f32[3,8,16,128]{3,2,1,0:T(8,128)} copy(f32[3,8,16,128]{3,2,1,0:T(8,128)S(1)} %copy-done) | data formatting | bytes 393216
Async XLA Ops:
  39.9 2.5 %copy-start = (f32[3,8,16,128]{3,2,1,0:T(8,128)S(1)}, f32[3,8,16,128]{3,2,1,0:T(8,128)}, u32[]{:S(2)}) copy-start(f32[3,8,16,128]{3,2,1,0:T(8,128)} %get-tuple-element.5) | copy-start | bytes 589828
